TPU v7x, 32 devices: a whole 2x2x4 slice. The times are simulated.
32 devices in a mesh: view: 4 (over y, core), slab: 8 (over z, x).
Axes of the slice: x: 2, y: 2, z: 4, core: 2. Of those that a mesh axis runs over, the one named last changes fastest.
Arguments:
- estimate: float32 [2, 128, 128, 1024], P(None, 'slab', 'view'), may hold values from 0.2 to 5
- recorded: bfloat16 [2, 2, 128, 128, 1024], P(None, None, None, 'view', 'slab'), may hold values from 0.19921875 to 5
- psf_lateral: float32 [2, 2, 31], replicated, may hold values from 0.0007 to 1.5, as said below
- psf_axial: float32 [2, 127], replicated, may hold values from 0.0007 to 1.5, as said below
- offsets: int32 [2, 2], replicated, may hold values from -8 to 8, as said below
Outputs:
- updated: float32 [2, 128, 128, 1024], P(None, 'slab', 'view')
Inputs may be any that keep to these rules, and one draw needn't show every extreme that they name: offsets[v] is imaging direction v's voxel shift along x and along y; the magnitude 8 occurs with both signs. `psf_lateral`: positive lateral taps. `psf_axial`: positive axial taps.
All inputs are finite; a program needn't handle non-finite values.
Results may differ from a plain program's by a relative error of at most 0.0003.
Values sent between devices are 32-bit elements; how exact they have to be, the bound alone decides.
No kernel may reach another device: no remote copies, remote signals or barrier semaphores. Data moves between devices by JAX's collectives and lax.ppermute only.
A program may use at most 128 MiB of HBM per device.

v0:
```python
import jax
import jax.numpy as jnp
from jax import lax
from jax.sharding import PartitionSpec as P

Z = 128
YBLK = 128
HALO = 23
BACKGROUND = 0.05
HIGHEST = lax.Precision.HIGHEST


def with_halo(value, sides, width):
    for axis, dim in sides:
        peers, length = (lax.axis_size(axis), value.shape[dim])
        up = [(i, (i + 1) % peers) for i in range(peers - 1)]
        down = [(j, i) for i, j in up]
        last = lax.slice_in_dim(value, length - width, length, axis=dim)
        leading = lax.slice_in_dim(value, 0, width, axis=dim)
        before = lax.ppermute(last, axis, up)
        after = lax.ppermute(leading, axis, down)
        value = jnp.concatenate([before, value, after], axis=dim)
    return value


def unit_taps(weights):
    return weights / jnp.sum(weights)


def band_table(weights, places):
    levels = jnp.arange(weights.shape[0], dtype=jnp.int32)
    return jnp.sum(jnp.where(places[..., None] == levels, weights, 0.0), axis=-1)


def margin_matrix(weights, offset, length, margin, adjoint):
    centre = (weights.shape[0] - 1) // 2
    outputs = jnp.arange(length, dtype=jnp.int32)[:, None]
    sources = jnp.arange(length + 2 * margin, dtype=jnp.int32)[None, :] - margin
    apart = sources - outputs
    if adjoint:
        apart = -apart
    return band_table(weights, apart - offset + centre)


def blocked_rows(field, weights, offset, width_blk, adjoint):
    extent = field.shape
    blocks = extent[3] // width_blk
    pieces = field.reshape(extent[0], extent[1], extent[2], blocks, width_blk)
    padded = jnp.pad(pieces, ((0, 0), (0, 0), (0, 0), (1, 1), (0, 0)))
    centre = (weights.shape[0] - 1) // 2
    sources = jnp.arange(width_blk, dtype=jnp.int32)[:, None]
    outputs = jnp.arange(width_blk, dtype=jnp.int32)[None, :]
    result = jnp.zeros(pieces.shape, jnp.float32)
    for shifted in range(3):
        apart = (shifted - 1) * width_blk + sources - outputs
        if adjoint:
            apart = -apart
        matrix = band_table(weights, apart - offset + centre)
        result = result + jnp.einsum(
            "czxkj,ji->czxki",
            padded[:, :, :, shifted : shifted + blocks],
            matrix,
            precision=HIGHEST,
        )
    return result.reshape(extent)


def shards(estimate, recorded, psf_lateral, psf_axial, offsets):
    views_n = recorded.shape[0]
    along_x = [unit_taps(psf_lateral[which, 0]) for which in range(views_n)]
    along_y = [unit_taps(psf_lateral[which, 1]) for which in range(views_n)]
    rows_at = jnp.arange(Z, dtype=jnp.int32)[:, None]
    cols_at = jnp.arange(Z, dtype=jnp.int32)[None, :]
    axial_places = cols_at - rows_at + (psf_axial.shape[1] - 1) // 2
    axial = [band_table(unit_taps(psf_axial[which]), axial_places) for which in range(views_n)]
    x_rows = estimate.shape[2]
    widened = with_halo(estimate, (("view", 2),), HALO)
    blurred = []
    for which in range(views_n):
        across = margin_matrix(along_x[which], offsets[which, 0], x_rows, HALO, False)
        sectioned = jnp.einsum("ab,czby->czay", across, widened, precision=HIGHEST)
        blurred.append(blocked_rows(sectioned, along_y[which], offsets[which, 1], YBLK, False))
    columns = lax.all_to_all(jnp.stack(blurred), "slab", split_axis=4, concat_axis=2, tiled=True)
    spread = []
    for which in range(views_n):
        imaged = jnp.einsum("oi,cixy->coxy", axial[which], columns[which], precision=HIGHEST)
        quotient = recorded[which].astype(jnp.float32) / (imaged + BACKGROUND)
        spread.append(jnp.einsum("oi,coxy->cixy", axial[which], quotient, precision=HIGHEST))
    planes = lax.all_to_all(jnp.stack(spread), "slab", split_axis=2, concat_axis=4, tiled=True)
    returned = [
        blocked_rows(planes[which], along_y[which], offsets[which, 1], YBLK, True)
        for which in range(views_n)
    ]
    fringe = with_halo(jnp.stack(returned), (("view", 3),), HALO)
    summed = jnp.zeros(estimate.shape, jnp.float32)
    for which in range(views_n):
        across = margin_matrix(along_x[which], offsets[which, 0], x_rows, HALO, True)
        summed = summed + jnp.einsum("ab,czby->czay", across, fringe[which], precision=HIGHEST)
    return estimate * (summed / views_n)


def solution(mesh):
    in_specs = (P(None, "slab", "view", None), P(None, None, None, "view", "slab"), P(), P(), P())
    out_specs = P(None, "slab", "view", None)
    return jax.shard_map(shards, mesh=mesh, in_specs=in_specs, out_specs=out_specs, check_vma=False)
```

profile of v0, /device:TPU:1, one launch (start us, length us, event | category | flops | bytes accessed | tf_op | source)
XLA Modules:
  0.0 831.5 jit_solution(896550517628313579)
XLA Ops:
  0.0 3.7 fusion.71
  5.5 4.5 collective-permute-start
  25.3 5.0 select_reduce_fusion.2
  30.3 12.5 %collective-permute-done = f32[2,16,23,1024]{3,1,2,0:T(8,128)S(1)} collective-permute-done((f32[2,16,23,1024]{3,1,2,0:T(8,128)S(1)}, f32[2,16,23,1024]{3,1,2,0:T(8,128)S(1)}, u32[]{:S(2)}, u32[]{:S(2)}) %collective-permute-start) | collective-permute-done | bytes 3014688 | tf_op jit(solution)/shard_map/ppermute | solution.py:20
  44.6 4.4 collective-permute-done.1
  50.7 11.1 %fusion.3 = f32[2,16,1024,32]{2,3,1,0:T(8,128)S(1)} fusion(f32[2,16,23,1024]{3,2,1,0:T(8,128)S(1)} %copy.64, f32[2,16,32,1024]{3,2,1,0:T(8,128)S(1)} %copy-done, f32[2,16,23,1024]{3,2,1,0:T(8,128)S(1)} %copy.63, f32[32,78]{1,0:T(8,128)S(1)} %get-tuple-element.61), kind=kOutput, calls=%fused_computation.21 | convolution fusion | flops 986578944 | bytes 14427904 | tf_op jit(solution)/shard_map/ab,czby->czay/dot_general | solution.py:81
  69.7 4.9 add_add_fusion.3
  74.6 5.3 stack_reshape.12
  79.9 13.7 %fusion.2 = f32[2,16,1024,32]{2,3,1,0:T(8,128)S(1)} fusion(f32[2,16,23,1024]{3,2,1,0:T(8,128)} %copy-done.4, f32[2,16,32,1024]{3,2,1,0:T(8,128)} %param.5, f32[2,16,23,1024]{3,2,1,0:T(8,128)S(1)} %copy.63, f32[32,78]{1,0:T(8,128)S(1)} %get-tuple-element.16), kind=kOutput, calls=%fused_computation.20 | convolution fusion | flops 986578944 | bytes 14427904 | tf_op jit(solution)/shard_map/ab,czby->czay/dot_general | solution.py:81
  101.4 4.9 add_add_fusion.2
  106.3 4.9 stack_reshape.13
  111.2 8.3 %pad_maximum_fusion.2 = f32[2,2,16,32,1024]{4,3,2,1,0:T(8,128)} fusion(f32[1,2,16,32,1024]{4,3,2,1,0:T(8,128)} %stack_reshape.13, f32[1,2,16,32,1024]{4,3,2,1,0:T(8,128)} %stack_reshape.12), kind=kLoop, calls=%fused_computation.14 | loop fusion | flops 2097152 | bytes 16777216 | tf_op jit(solution)/shard_map/stack | solution.py:83
  119.6 26.6 %copy.65 = f32[2,2,16,32,1024]{3,2,1,0,4:T(8,128)} copy(f32[2,2,16,32,1024]{4,3,2,1,0:T(8,128)} %pad_maximum_fusion.2) | data formatting | bytes 16777216 | tf_op jit(solution)/shard_map/stack | solution.py:83
  146.1 20.5 %reshape.373 = f32[8,1,262144]{2,1,0:T(1,128)} reshape(f32[1024,2,2,16,32]{4,3,2,1,0:T(8,128)} %bitcast.192) | data formatting | bytes 16777216
  166.6 5.5 all-to-all-start
  172.2 4.4 fusion.70
  176.6 4.6 copy.100
  187.9 150.7 %all-to-all-done = f32[8,1,262144]{2,1,0:T(1,128)} async-done(((f32[8,1,262144]{2,1,0:T(1,128)}), f32[8,1,262144]{2,1,0:T(1,128)}, u32[]{:S(2)}, u32[]{:S(2)}) %all-to-all-start) | async-done | bytes 8388640 | tf_op jit(solution)/shard_map/all_to_all | solution.py:83
  339.1 26.4 %reduce.6 = f32[8,262144]{1,0:T(8,128)} reduce(f32[8,1,262144]{2,1,0:T(1,128)} %all-to-all-done, f32[]{:T(128)} %broadcast.385), dimensions={1}, to_apply=%all_to_all.22.reduce_sub_computation | reduce | bytes 16777220 | tf_op jit(solution)/shard_map/all_to_all | solution.py:83
  365.5 25.3 %reshape.374 = f32[1024,2,2,16,32]{4,3,2,1,0:T(8,128)} reshape(f32[8,262144]{1,0:T(8,128)} %reduce.6) | data formatting | bytes 16777216
  390.7 18.4 %copy.97 = f32[2,2,16,32,8,128]{5,4,3,2,1,0:T(8,128)} copy(f32[2,2,16,32,8,128]{3,2,1,0,5,4:T(8,128)} %bitcast.193) | data formatting | bytes 16777216 | tf_op jit(solution)/shard_map/all_to_all | solution.py:83
  409.1 4.0 fusion.69
  414.8 8.4 %fusion.18 = f32[2,32,128,128]{3,2,1,0:T(8,128)S(1)} fusion(f32[2,128,32,128]{3,2,1,0:T(8,128)S(1)} %bitcast.206, f32[128,128]{1,0:T(8,128)S(1)} %get-tuple-element.5), kind=kOutput, calls=%fused_computation.41 | convolution fusion | flops 1610612736 | bytes 8454144 | tf_op jit(solution)/shard_map/oi,cixy->coxy/dot_general | solution.py:86
  423.2 4.1 fusion.22
  427.3 8.4 %fusion.16 = f32[2,32,128,128]{3,2,1,0:T(8,128)S(1)} fusion(f32[2,128,32,128]{3,2,1,0:T(8,128)S(1)} %bitcast.205, f32[128,128]{1,0:T(8,128)S(1)} %get-tuple-element.6), kind=kOutput, calls=%fused_computation.39 | convolution fusion | flops 1610612736 | bytes 8454144 | tf_op jit(solution)/shard_map/oi,cixy->coxy/dot_general | solution.py:86
  435.7 4.3 fusion.23
  440.0 3.8 pad_maximum_fusion.3
  443.8 10.3 %copy.72 = f32[2,2,128,32,128]{4,3,1,0,2:T(8,128)} copy(f32[2,2,128,32,128]{2,4,3,1,0:T(8,128)} %pad_maximum_fusion.3) | data formatting | bytes 16777216 | tf_op jit(solution)/shard_map/stack | solution.py:89
  454.1 187.0 %all_to_all.30 = f32[2,2,128,32,128]{4,3,1,0,2:T(8,128)S(1)} all-to-all(f32[2,2,128,32,128]{4,3,1,0,2:T(8,128)} %copy.72), channel_id=1, replica_groups=mesh['view'=4,'slab'=8] {'slab'}, dimensions={2} | all-to-all | bytes 16777216 | tf_op jit(solution)/shard_map/all_to_all | solution.py:89
  641.1 8.1 copy.111
  653.7 3.6 fusion.29
  660.8 4.9 add_add_fusion
  665.7 4.9 stack_reshape.15
  670.6 5.3 fusion.33
  679.5 5.1 add_add_fusion.1
  684.6 4.9 stack_reshape.14
  689.5 4.8 constant_dynamic-update-slice_fusion.1
  696.6 9.5 %fusion.68 = (f32[2,2,16,23,1024]{4,3,2,1,0:T(8,128)}, f32[2,2,16,23,1024]{4,3,2,1,0:T(8,128)S(1)}) fusion(f32[2,2,16,32,1024]{4,3,2,1,0:T(8,128)} %constant_dynamic-update-slice_fusion), kind=kLoop, calls=%fused_computation.165 | loop fusion | bytes 24117248 | tf_op jit(solution)/shard_map/slice | solution.py:18
  706.2 6.3 copy.75
  712.4 4.0 collective-permute-start.2
  716.4 3.5 copy.76
  721.8 59.3 %collective-permute-done.2 = f32[2,2,16,23,1024]{4,2,3,1,0:T(8,128)S(1)} collective-permute-done((f32[2,2,16,23,1024]{4,2,3,1,0:T(8,128)S(1)}, f32[2,2,16,23,1024]{4,2,3,1,0:T(8,128)S(1)}, u32[]{:S(2)}, u32[]{:S(2)}) %collective-permute-start.2) | collective-permute-done | bytes 6029344 | tf_op jit(solution)/shard_map/ppermute | solution.py:20
  781.1 3.5 copy.77
  784.6 4.8 collective-permute-done.3
  789.4 6.2 copy.78
  795.6 8.4 %pad_maximum_fusion = f32[2,2,16,78,1024]{4,3,2,1,0:T(8,128)S(1)} fusion(f32[2,2,16,23,1024]{4,3,2,1,0:T(8,128)} %copy.78, f32[2,2,16,32,1024]{4,3,2,1,0:T(8,128)} %constant_dynamic-update-slice_fusion, f32[2,2,16,23,1024]{4,3,2,1,0:T(8,128)S(1)} %copy.77), kind=kLoop, calls=%fused_computation | loop fusion | flops 10223616 | bytes 40894464 | tf_op jit(solution)/shard_map/concatenate | solution.py:22
  804.1 12.3 %fusion = f32[2,16,1024,32]{2,3,1,0:T(8,128)} fusion(f32[2,2,16,78,1024]{4,3,2,1,0:T(8,128)S(1)} %pad_maximum_fusion, f32[32,78]{1,0:T(8,128)S(1)} %copy-done.15), kind=kOutput, calls=%fused_computation.2 | convolution fusion | flops 981467136 | bytes 14696448 | tf_op jit(solution)/shard_map/ab,czby->czay/dot_general | solution.py:98
  816.4 14.9 %bitcast_multiply_fusion = f32[2,16,32,1024]{3,2,1,0:T(8,128)} fusion(f32[2,16,32,1024]{3,2,1,0:T(8,128)S(1)} %copy-done.1, f32[2,16,1024,32]{2,3,1,0:T(8,128)} %fusion, f32[2,2,16,78,1024]{4,3,2,1,0:T(8,128)S(1)} %pad_maximum_fusion, f32[32,78]{1,0:T(8,128)S(1)} %copy-done.14), kind=kOutput, calls=%fused_computation.36 | convolution fusion | flops 984612864 | bytes 23085056 | tf_op jit(solution)/shard_map/ab,czby->czay/dot_general | solution.py:98
  (76 shorter events, 60.5 us)
Async XLA Ops:
  5.5 8.3 copy-start.18
  5.5 9.0 %copy-start.16 = (f32[2,2,31]{2,1,0:T(2,128)S(1)}, f32[2,2,31]{2,1,0:T(2,128)}, u32[]{:S(2)}) copy-start(f32[2,2,31]{2,1,0:T(2,128)} %param.7) | copy-start | bytes 1492
  5.5 37.3 %collective-permute-start = (f32[2,16,23,1024]{3,1,2,0:T(8,128)S(1)}, f32[2,16,23,1024]{3,1,2,0:T(8,128)S(1)}, u32[]{:S(2)}, u32[]{:S(2)}) collective-permute-start(f32[2,16,23,1024]{3,1,2,0:T(8,128)S(1)} %copy.101), channel_id=1, source_target_pairs={{0,8},{8,16},{16,24},{1,9},{9,17},{17,25},{2,10},{10,18},{18,26},{... | collective-permute-start | bytes 9043976 | tf_op jit(solution)/shard_map/ppermute | solution.py:20
  11.8 37.2 %collective-permute-start.1 = (f32[2,16,23,1024]{3,1,2,0:T(8,128)S(1)}, f32[2,16,23,1024]{3,1,2,0:T(8,128)S(1)}, u32[]{:S(2)}, u32[]{:S(2)}) collective-permute-start(f32[2,16,23,1024]{3,1,2,0:T(8,128)S(1)} %copy.102), channel_id=1, source_target_pairs={{8,0},{16,8},{24,16},{9,1},{17,9},{25,17},{10,2},{18,10},{26,18},{... | collective-permute-start | bytes 9043976 | tf_op jit(solution)/shard_map/ppermute | solution.py:21
  44.6 6.2 copy-start
  50.7 11.1 %copy-start.4 = (f32[2,16,23,1024]{3,2,1,0:T(8,128)}, f32[2,16,23,1024]{3,2,1,0:T(8,128)S(1)}, u32[]{:S(2)}) copy-start(f32[2,16,23,1024]{3,2,1,0:T(8,128)S(1)} %copy.64) | copy-start | bytes 9043972
  166.6 172.0 %all-to-all-start = ((f32[8,1,262144]{2,1,0:T(1,128)}), f32[8,1,262144]{2,1,0:T(1,128)}, u32[]{:S(2)}, u32[]{:S(2)}) async-start(f32[8,1,262144]{2,1,0:T(1,128)} %reshape.373), calls=%async_computation | async-start | bytes 16777216 | tf_op jit(solution)/shard_map/all_to_all | solution.py:83
  176.6 7.5 copy-start.17
  414.8 8.4 %copy-start.7 = (bf16[1,2,128,32,128]{2,4,3,1,0:T(8,128)(2,1)S(1)}, bf16[1,2,128,32,128]{2,4,3,1,0:T(8,128)(2,1)}, u32[]{:S(2)}) copy-start(bf16[1,2,128,32,128]{2,4,3,1,0:T(8,128)(2,1)} %copy.100) | copy-start | bytes 6291460
  427.3 8.4 %copy-start.6 = (bf16[1,2,128,32,128]{2,4,3,1,0:T(8,128)(2,1)S(1)}, bf16[1,2,128,32,128]{2,4,3,1,0:T(8,128)(2,1)}, u32[]{:S(2)}) copy-start(bf16[1,2,128,32,128]{2,4,3,1,0:T(8,128)(2,1)} %copy.103) | copy-start | bytes 6291460
  649.2 4.5 copy-start.2
  649.2 4.5 copy-start.13
  653.7 3.6 copy-start.12
  657.3 3.4 copy-start.11
  665.7 4.9 copy-start.10
  670.6 5.4 copy-start.3
  670.6 5.4 copy-start.9
  676.0 3.4 copy-start.8
  689.5 4.9 copy-start.5
  712.4 68.7 %collective-permute-start.2 = (f32[2,2,16,23,1024]{4,2,3,1,0:T(8,128)S(1)}, f32[2,2,16,23,1024]{4,2,3,1,0:T(8,128)S(1)}, u32[]{:S(2)}, u32[]{:S(2)}) collective-permute-start(f32[2,2,16,23,1024]{4,2,3,1,0:T(8,128)S(1)} %copy.75), channel_id=1, source_target_pairs={{0,8},{8,16},{16,24},{1,9},{9,17},{17,25},{2,10},{10,18},{18,26},{... | collective-permute-start | bytes 18087944 | tf_op jit(solution)/shard_map/ppermute | solution.py:20
  719.9 69.5 %collective-permute-start.3 = (f32[2,2,16,23,1024]{4,2,3,1,0:T(8,128)S(1)}, f32[2,2,16,23,1024]{4,2,3,1,0:T(8,128)S(1)}, u32[]{:S(2)}, u32[]{:S(2)}) collective-permute-start(f32[2,2,16,23,1024]{4,2,3,1,0:T(8,128)S(1)} %copy.76), channel_id=1, source_target_pairs={{8,0},{16,8},{24,16},{9,1},{17,9},{25,17},{10,2},{18,10},{26,18},{... | collective-permute-start | bytes 18087944 | tf_op jit(solution)/shard_map/ppermute | solution.py:21
  795.6 8.4 %copy-start.15 = (f32[32,78]{1,0:T(8,128)S(1)}, f32[32,78]{1,0:T(8,128)}, u32[]{:S(2)}) copy-start(f32[32,78]{1,0:T(8,128)} %get-tuple-element.15) | copy-start | bytes 29956
  804.0 12.3 %copy-start.1 = (f32[2,16,32,1024]{3,2,1,0:T(8,128)S(1)}, f32[2,16,32,1024]{3,2,1,0:T(8,128)}, u32[]{:S(2)}) copy-start(f32[2,16,32,1024]{3,2,1,0:T(8,128)} %param.5) | copy-start | bytes 12582916
  804.1 12.3 %copy-start.14 = (f32[32,78]{1,0:T(8,128)S(1)}, f32[32,78]{1,0:T(8,128)}, u32[]{:S(2)}) copy-start(f32[32,78]{1,0:T(8,128)} %get-tuple-element.62) | copy-start | bytes 29956
where the time goes:
time: 839 us; the launch traced here: 831 us
  waiting for transfers between devices  232 us (28%)
  local copies, waits for them, and re-layouts  201 us (24%)
  blocking collectives  187 us (22%)
  matrix products  126 us (15%)
  other arithmetic  66.6 us (8%)
  starting transfers between devices  17.9 us (2%)
    all_to_all x1, blocking collectives, shards(): lax.all_to_all(jnp.stack(spread), 'slab', split_axis=2, concat_axis=4, ti...  187 us
    all_to_all x1, waiting for transfers between devices, shards(): lax.all_to_all(jnp.stack(blurred), 'slab', split_axis=4, concat_axis=2, t...  151 us
    ppermute x2, waiting for transfers between devices, with_halo(): before = lax.ppermute(last, axis, up)  71.8 us
    unnamed x47, local copies, waits for them, and re-layouts  65 us
    dot_general x12, matrix products, blocked_rows(): jnp.einsum('czxkj,ji->czxki', padded[:, :, :, shifted:shifted + blocks],...  49.3 us
    another operation x3, local copies, waits for them, and re-layouts, shards(): jnp.stack(blurred)  36.7 us
    dot_general x2, matrix products, shards(): jnp.einsum('ab,czby->czay', across, fringe[which], precision=HIGHEST)  27.2 us
    all_to_all x1, other arithmetic, shards(): lax.all_to_all(jnp.stack(blurred), 'slab', split_axis=4, concat_axis=2, t...  26.4 us
  transfers between devices with their start and end apart: 5, of which 5 were waited for; matrix products, arithmetic and copies ran while one was open for 5% of the time, Pallas kernels for 0%

commit v1 on v0

--- a/solution.py
+++ b/solution.py
@@ -8,6 +8,17 @@
 HALO = 23
 BACKGROUND = 0.05
 HIGHEST = lax.Precision.HIGHEST
+
+
+def split_up(array, dim, count):
+    before, after = (array.shape[:dim], array.shape[dim + 1 :])
+    return jnp.moveaxis(array.reshape(*before, count, -1, *after), dim, 0)
+
+
+def in_order(pieces, dim):
+    shape = list(pieces.shape[1:])
+    shape[dim] *= pieces.shape[0]
+    return jnp.moveaxis(pieces, 0, dim).reshape(shape)
 
 
 def with_halo(value, sides, width):
@@ -86,7 +97,17 @@
         imaged = jnp.einsum("oi,cixy->coxy", axial[which], columns[which], precision=HIGHEST)
         quotient = recorded[which].astype(jnp.float32) / (imaged + BACKGROUND)
         spread.append(jnp.einsum("oi,coxy->cixy", axial[which], quotient, precision=HIGHEST))
-    planes = lax.all_to_all(jnp.stack(spread), "slab", split_axis=2, concat_axis=4, tiled=True)
+    x = jnp.stack(spread)
+    devices, mine = (lax.axis_size("slab"), lax.axis_index("slab"))
+    tiles = split_up(x, 2, devices)
+    gathered = [tiles[mine]]
+    for step in range(1, devices):
+        sent = tiles[(mine + step) % devices]
+        gathered.append(
+            lax.ppermute(sent, "slab", [(i_2, (i_2 + step) % devices) for i_2 in range(devices)])
+        )
+    tiles = jnp.stack(gathered)[(mine - jnp.arange(devices)) % devices]
+    planes = in_order(tiles, 4)
     returned = [
         blocked_rows(planes[which], along_y[which], offsets[which, 1], YBLK, True)
         for which in range(views_n)

time: 839 us -> 838 us (level)
  the two profiles are of different devices: /device:TPU:1 before, /device:TPU:25 now
where the time goes in v1:
time: 838 us; the launch traced here: 831 us
  waiting for transfers between devices  283 us (34%)
  local copies, waits for them, and re-layouts  221 us (26%)
  starting transfers between devices  132 us (16%)
  matrix products  129 us (15%)
  other arithmetic  65.3 us (8%)
    all_to_all x1, waiting for transfers between devices, shards(): lax.all_to_all(jnp.stack(blurred), 'slab', split_axis=4, concat_axis=2, t...  149 us
    ppermute x7, starting transfers between devices, shards(): lax.ppermute(sent, 'slab', [(i_2, (i_2 + step) % devices) for i_2 in rang...  115 us
    unnamed x58, local copies, waits for them, and re-layouts  77.6 us
    ppermute x2, waiting for transfers between devices, with_halo(): before = lax.ppermute(last, axis, up)  71.8 us
    ppermute x7, waiting for transfers between devices, shards(): lax.ppermute(sent, 'slab', [(i_2, (i_2 + step) % devices) for i_2 in rang...  53.6 us
    dot_general x12, matrix products, blocked_rows(): jnp.einsum('czxkj,ji->czxki', padded[:, :, :, shifted:shifted + blocks],...  49.1 us
    another operation x3, local copies, waits for them, and re-layouts, shards(): jnp.stack(blurred)  36.7 us
    dot_general x2, matrix products, shards(): jnp.einsum('ab,czby->czay', across, fringe[which], precision=HIGHEST)  27.2 us
  transfers between devices with their start and end apart: 12, of which 8 were waited for; matrix products, arithmetic and copies ran while one was open for 7% of the time, Pallas kernels for 0%

profile of v1, /device:TPU:25, one launch (start us, length us, event | category | flops | bytes accessed | tf_op | source)
XLA Modules:
  0.0 830.7 jit_solution(13230410909537027715)
XLA Ops:
  0.0 3.7 fusion.79
  5.5 3.7 collective-permute-start
  24.4 5.0 select_reduce_fusion.2
  29.5 12.5 %collective-permute-done = f32[2,16,23,1024]{3,1,2,0:T(8,128)S(1)} collective-permute-done((f32[2,16,23,1024]{3,1,2,0:T(8,128)S(1)}, f32[2,16,23,1024]{3,1,2,0:T(8,128)S(1)}, u32[]{:S(2)}, u32[]{:S(2)}) %collective-permute-start) | collective-permute-done | bytes 3014688 | tf_op jit(solution)/shard_map/ppermute | solution.py:31
  43.7 4.4 collective-permute-done.1
  49.9 11.1 %fusion.3 = f32[2,16,1024,32]{2,3,1,0:T(8,128)S(1)} fusion(f32[2,16,23,1024]{3,2,1,0:T(8,128)S(1)} %copy.101, f32[2,16,32,1024]{3,2,1,0:T(8,128)S(1)} %copy-done, f32[2,16,23,1024]{3,2,1,0:T(8,128)S(1)} %copy.100, f32[32,78]{1,0:T(8,128)S(1)} %get-tuple-element.69), kind=kOutput, calls=%fused_computation.37 | convolution fusion | flops 986578944 | bytes 14427904 | tf_op jit(solution)/shard_map/ab,czby->czay/dot_general | solution.py:92
  68.9 4.9 add_add_fusion.3
  73.8 5.3 stack_reshape.12
  79.1 13.7 %fusion.2 = f32[2,16,1024,32]{2,3,1,0:T(8,128)S(1)} fusion(f32[2,16,23,1024]{3,2,1,0:T(8,128)} %copy-done.4, f32[2,16,32,1024]{3,2,1,0:T(8,128)} %param.5, f32[2,16,23,1024]{3,2,1,0:T(8,128)S(1)} %copy.100, f32[32,78]{1,0:T(8,128)S(1)} %get-tuple-element.16), kind=kOutput, calls=%fused_computation.36 | convolution fusion | flops 986578944 | bytes 14427904 | tf_op jit(solution)/shard_map/ab,czby->czay/dot_general | solution.py:92
  100.6 4.9 add_add_fusion.2
  105.5 4.9 stack_reshape.13
  110.4 8.3 %pad_maximum_fusion.2 = f32[2,2,16,32,1024]{4,3,2,1,0:T(8,128)} fusion(f32[1,2,16,32,1024]{4,3,2,1,0:T(8,128)} %stack_reshape.13, f32[1,2,16,32,1024]{4,3,2,1,0:T(8,128)} %stack_reshape.12), kind=kLoop, calls=%fused_computation.31 | loop fusion | flops 2097152 | bytes 16777216 | tf_op jit(solution)/shard_map/stack | solution.py:94
  118.7 26.6 %copy.102 = f32[2,2,16,32,1024]{3,2,1,0,4:T(8,128)} copy(f32[2,2,16,32,1024]{4,3,2,1,0:T(8,128)} %pad_maximum_fusion.2) | data formatting | bytes 16777216 | tf_op jit(solution)/shard_map/stack | solution.py:94
  145.3 20.5 %reshape.453 = f32[8,1,262144]{2,1,0:T(1,128)} reshape(f32[1024,2,2,16,32]{4,3,2,1,0:T(8,128)} %bitcast.226) | data formatting | bytes 16777216
  165.8 5.5 all-to-all-start
  171.3 4.4 fusion.78
  175.7 4.6 copy.154
  187.0 149.0 %all-to-all-done = f32[8,1,262144]{2,1,0:T(1,128)} async-done(((f32[8,1,262144]{2,1,0:T(1,128)}), f32[8,1,262144]{2,1,0:T(1,128)}, u32[]{:S(2)}, u32[]{:S(2)}) %all-to-all-start) | async-done | bytes 8388640 | tf_op jit(solution)/shard_map/all_to_all | solution.py:94
  336.4 26.4 %reduce.6 = f32[8,262144]{1,0:T(8,128)} reduce(f32[8,1,262144]{2,1,0:T(1,128)} %all-to-all-done, f32[]{:T(128)} %broadcast.461), dimensions={1}, to_apply=%all_to_all.11.reduce_sub_computation | reduce | bytes 16777220 | tf_op jit(solution)/shard_map/all_to_all | solution.py:94
  362.8 25.3 %reshape.454 = f32[1024,2,2,16,32]{4,3,2,1,0:T(8,128)} reshape(f32[8,262144]{1,0:T(8,128)} %reduce.6) | data formatting | bytes 16777216
  388.1 18.4 %copy.148 = f32[2,2,16,32,8,128]{5,4,3,2,1,0:T(8,128)} copy(f32[2,2,16,32,8,128]{3,2,1,0,5,4:T(8,128)} %bitcast.227) | data formatting | bytes 16777216 | tf_op jit(solution)/shard_map/all_to_all | solution.py:94
  406.5 4.0 fusion.77
  412.1 8.8 %fusion.16 = f32[2,32,128,128]{3,2,1,0:T(8,128)S(1)} fusion(f32[2,128,32,128]{3,2,1,0:T(8,128)S(1)} %bitcast.239, f32[128,128]{1,0:T(8,128)S(1)} %get-tuple-element.5), kind=kOutput, calls=%fused_computation.55 | convolution fusion | flops 1610612736 | bytes 8454144 | tf_op jit(solution)/shard_map/oi,cixy->coxy/dot_general | solution.py:97
  420.9 5.0 fusion.12
  425.9 9.0 %fusion.18 = f32[2,32,128,128]{3,2,1,0:T(8,128)S(1)} fusion(f32[2,128,32,128]{3,2,1,0:T(8,128)S(1)} %bitcast.238, f32[128,128]{1,0:T(8,128)S(1)} %get-tuple-element.6), kind=kOutput, calls=%fused_computation.57 | convolution fusion | flops 1610612736 | bytes 8454144 | tf_op jit(solution)/shard_map/oi,cixy->coxy/dot_general | solution.py:97
  435.0 4.9 fusion.13
  456.0 13.4 %collective-permute-done.2 = f32[2,2,16,32,128]{4,3,2,1,0:T(8,128)} collective-permute-done((f32[2,2,16,32,128]{4,3,2,1,0:T(8,128)}, f32[2,2,16,32,128]{4,3,2,1,0:T(8,128)}, u32[]{:S(2)}, u32[]{:S(2)}) %collective-permute-start.2) | collective-permute-done | bytes 1048608 | tf_op jit(solution)/shard_map/ppermute | solution.py:107
  471.6 109.7 %collective-permute-start.8 = (f32[2,2,16,32,128]{4,3,2,1,0:T(8,128)S(1)}, f32[2,2,16,32,128]{4,3,2,1,0:T(8,128)S(1)}, u32[]{:S(2)}, u32[]{:S(2)}) collective-permute-start(f32[2,2,16,32,128]{4,3,2,1,0:T(8,128)S(1)} %bitcast.247), channel_id=1, source_target_pairs={{0,7},{1,0},{2,1},{3,2},{4,3},{5,4},{6,5},{7,6},{8,15},{9,8},{10,9... | collective-permute-start | bytes 3145736 | tf_op jit(solution)/shard_map/ppermute | solution.py:107
  583.6 19.5 %collective-permute-done.4 = f32[2,2,16,32,128]{4,3,2,1,0:T(8,128)} collective-permute-done((f32[2,2,16,32,128]{4,3,2,1,0:T(8,128)}, f32[2,2,16,32,128]{4,3,2,1,0:T(8,128)}, u32[]{:S(2)}, u32[]{:S(2)}) %collective-permute-start.4) | collective-permute-done | bytes 1048608 | tf_op jit(solution)/shard_map/ppermute | solution.py:107
  605.3 20.7 %collective-permute-done.5 = f32[2,2,16,32,128]{4,3,2,1,0:T(8,128)S(1)} collective-permute-done((f32[2,2,16,32,128]{4,3,2,1,0:T(8,128)S(1)}, f32[2,2,16,32,128]{4,3,2,1,0:T(8,128)S(1)}, u32[]{:S(2)}, u32[]{:S(2)}) %collective-permute-start.5) | collective-permute-done | bytes 1048608 | tf_op jit(solution)/shard_map/ppermute | solution.py:107
  630.3 7.7 gather_fusion
  638.0 11.5 %copy.170 = f32[8,2,2,16,32,128]{5,0,4,3,2,1:T(8,128)S(1)} copy(f32[8,2,2,16,32,128]{5,4,3,2,1,0:T(8,128)} %gather_fusion) | data formatting | bytes 16777216 | tf_op jit(solution)/shard_map/gather | solution.py:109
  654.0 3.6 fusion.35
  661.1 4.9 add_add_fusion
  666.0 4.9 stack_reshape.15
  670.9 5.3 fusion.39
  679.7 4.9 add_add_fusion.1
  684.7 5.1 stack_reshape.14
  689.8 4.9 constant_dynamic-update-slice_fusion.1
  696.9 9.5 %fusion.76 = (f32[2,2,16,23,1024]{4,3,2,1,0:T(8,128)}, f32[2,2,16,23,1024]{4,3,2,1,0:T(8,128)S(1)}) fusion(f32[2,2,16,32,1024]{4,3,2,1,0:T(8,128)} %constant_dynamic-update-slice_fusion), kind=kLoop, calls=%fused_computation.209 | loop fusion | bytes 24117248 | tf_op jit(solution)/shard_map/slice | solution.py:29
  706.4 6.3 copy.122
  715.6 3.5 copy.123
  721.5 59.3 %collective-permute-done.9 = f32[2,2,16,23,1024]{4,2,3,1,0:T(8,128)S(1)} collective-permute-done((f32[2,2,16,23,1024]{4,2,3,1,0:T(8,128)S(1)}, f32[2,2,16,23,1024]{4,2,3,1,0:T(8,128)S(1)}, u32[]{:S(2)}, u32[]{:S(2)}) %collective-permute-start.9) | collective-permute-done | bytes 6029344 | tf_op jit(solution)/shard_map/ppermute | solution.py:31
  784.2 4.4 collective-permute-done.10
  788.6 6.2 copy.125
  794.8 8.4 %pad_maximum_fusion = f32[2,2,16,78,1024]{4,3,2,1,0:T(8,128)S(1)} fusion(f32[2,2,16,23,1024]{4,3,2,1,0:T(8,128)} %copy.125, f32[2,2,16,32,1024]{4,3,2,1,0:T(8,128)} %constant_dynamic-update-slice_fusion, f32[2,2,16,23,1024]{4,3,2,1,0:T(8,128)S(1)} %copy.124), kind=kLoop, calls=%fused_computation.1 | loop fusion | flops 10223616 | bytes 40894464 | tf_op jit(solution)/shard_map/concatenate | solution.py:33
  803.3 12.3 %fusion = f32[2,16,1024,32]{2,3,1,0:T(8,128)} fusion(f32[2,2,16,78,1024]{4,3,2,1,0:T(8,128)S(1)} %pad_maximum_fusion, f32[32,78]{1,0:T(8,128)S(1)} %copy-done.17), kind=kOutput, calls=%fused_computation.19 | convolution fusion | flops 981467136 | bytes 14696448 | tf_op jit(solution)/shard_map/ab,czby->czay/dot_general | solution.py:119
  815.6 14.9 %bitcast_multiply_fusion = f32[2,16,32,1024]{3,2,1,0:T(8,128)} fusion(f32[2,16,32,1024]{3,2,1,0:T(8,128)S(1)} %copy-done.1, f32[2,16,1024,32]{2,3,1,0:T(8,128)} %fusion, f32[2,2,16,78,1024]{4,3,2,1,0:T(8,128)S(1)} %pad_maximum_fusion, f32[32,78]{1,0:T(8,128)S(1)} %copy-done.16), kind=kOutput, calls=%fused_computation.52 | convolution fusion | flops 984612864 | bytes 23085056 | tf_op jit(solution)/shard_map/ab,czby->czay/dot_general | solution.py:119
  (111 shorter events, 94.5 us)
Async XLA Ops:
  5.5 7.5 copy-start.20
  5.5 8.1 copy-start.18
  5.5 36.5 %collective-permute-start = (f32[2,16,23,1024]{3,1,2,0:T(8,128)S(1)}, f32[2,16,23,1024]{3,1,2,0:T(8,128)S(1)}, u32[]{:S(2)}, u32[]{:S(2)}) collective-permute-start(f32[2,16,23,1024]{3,1,2,0:T(8,128)S(1)} %copy.152), channel_id=1, source_target_pairs={{0,8},{8,16},{16,24},{1,9},{9,17},{17,25},{2,10},{10,18},{18,26},{... | collective-permute-start | bytes 9043976 | tf_op jit(solution)/shard_map/ppermute | solution.py:31
  10.9 37.2 %collective-permute-start.1 = (f32[2,16,23,1024]{3,1,2,0:T(8,128)S(1)}, f32[2,16,23,1024]{3,1,2,0:T(8,128)S(1)}, u32[]{:S(2)}, u32[]{:S(2)}) collective-permute-start(f32[2,16,23,1024]{3,1,2,0:T(8,128)S(1)} %copy.153), channel_id=1, source_target_pairs={{8,0},{16,8},{24,16},{9,1},{17,9},{25,17},{10,2},{18,10},{26,18},{... | collective-permute-start | bytes 9043976 | tf_op jit(solution)/shard_map/ppermute | solution.py:32
  43.7 6.2 copy-start
  49.9 11.1 %copy-start.4 = (f32[2,16,23,1024]{3,2,1,0:T(8,128)}, f32[2,16,23,1024]{3,2,1,0:T(8,128)S(1)}, u32[]{:S(2)}) copy-start(f32[2,16,23,1024]{3,2,1,0:T(8,128)S(1)} %copy.101) | copy-start | bytes 9043972
  165.8 170.2 %all-to-all-start = ((f32[8,1,262144]{2,1,0:T(1,128)}), f32[8,1,262144]{2,1,0:T(1,128)}, u32[]{:S(2)}, u32[]{:S(2)}) async-start(f32[8,1,262144]{2,1,0:T(1,128)} %reshape.453), calls=%async_computation | async-start | bytes 16777216 | tf_op jit(solution)/shard_map/all_to_all | solution.py:94
  175.7 7.5 copy-start.19
  412.1 8.8 %copy-start.9 = (bf16[1,2,128,32,128]{2,4,3,1,0:T(8,128)(2,1)S(1)}, bf16[1,2,128,32,128]{2,4,3,1,0:T(8,128)(2,1)}, u32[]{:S(2)}) copy-start(bf16[1,2,128,32,128]{2,4,3,1,0:T(8,128)(2,1)} %copy.154) | copy-start | bytes 6291460
  425.9 13.9 %copy-start.6 = (f32[2,32,128,128]{2,3,1,0:T(8,128)}, f32[2,32,128,128]{2,3,1,0:T(8,128)S(1)}, u32[]{:S(2)}) copy-start(f32[2,32,128,128]{2,3,1,0:T(8,128)S(1)} %fusion.12) | copy-start | bytes 12582916
  425.9 9.0 %copy-start.8 = (bf16[1,2,128,32,128]{2,4,3,1,0:T(8,128)(2,1)S(1)}, bf16[1,2,128,32,128]{2,4,3,1,0:T(8,128)(2,1)}, u32[]{:S(2)}) copy-start(bf16[1,2,128,32,128]{2,4,3,1,0:T(8,128)(2,1)} %copy.151) | copy-start | bytes 6291460
  439.8 2.0 copy-start.7
  443.2 26.2 %collective-permute-start.2 = (f32[2,2,16,32,128]{4,3,2,1,0:T(8,128)}, f32[2,2,16,32,128]{4,3,2,1,0:T(8,128)}, u32[]{:S(2)}, u32[]{:S(2)}) collective-permute-start(f32[2,2,16,32,128]{4,3,2,1,0:T(8,128)} %bitcast.225), channel_id=1, source_target_pairs={{0,1},{1,2},{2,3},{3,4},{4,5},{5,6},{6,7},{7,0},{8,9},{9,10},{10,1... | collective-permute-start | bytes 3145736 | tf_op jit(solution)/shard_map/ppermute | solution.py:107
  445.0 26.6 %collective-permute-start.3 = (f32[2,2,16,32,128]{4,3,2,1,0:T(8,128)}, f32[2,2,16,32,128]{4,3,2,1,0:T(8,128)}, u32[]{:S(2)}, u32[]{:S(2)}) collective-permute-start(f32[2,2,16,32,128]{4,3,2,1,0:T(8,128)} %bitcast.224), channel_id=1, source_target_pairs={{0,2},{1,3},{2,4},{3,5},{4,6},{5,7},{6,0},{7,1},{8,10},{9,11},{10,... | collective-permute-start | bytes 3145736 | tf_op jit(solution)/shard_map/ppermute | solution.py:107
  448.2 154.8 %collective-permute-start.4 = (f32[2,2,16,32,128]{4,3,2,1,0:T(8,128)}, f32[2,2,16,32,128]{4,3,2,1,0:T(8,128)}, u32[]{:S(2)}, u32[]{:S(2)}) collective-permute-start(f32[2,2,16,32,128]{4,3,2,1,0:T(8,128)} %bitcast.223), channel_id=1, source_target_pairs={{0,3},{1,4},{2,5},{3,6},{4,7},{5,0},{6,1},{7,2},{8,11},{9,12},{10,... | collective-permute-start | bytes 3145736 | tf_op jit(solution)/shard_map/ppermute | solution.py:107
  450.4 176.7 %collective-permute-start.6 = (f32[2,2,16,32,128]{4,3,2,1,0:T(8,128)S(1)}, f32[2,2,16,32,128]{4,3,2,1,0:T(8,128)S(1)}, u32[]{:S(2)}, u32[]{:S(2)}) collective-permute-start(f32[2,2,16,32,128]{4,3,2,1,0:T(8,128)S(1)} %bitcast.246), channel_id=1, source_target_pairs={{0,5},{1,6},{2,7},{3,0},{4,1},{5,2},{6,3},{7,4},{8,13},{9,14},{10,... | collective-permute-start | bytes 3145736 | tf_op jit(solution)/shard_map/ppermute | solution.py:107
  453.9 172.2 %collective-permute-start.5 = (f32[2,2,16,32,128]{4,3,2,1,0:T(8,128)S(1)}, f32[2,2,16,32,128]{4,3,2,1,0:T(8,128)S(1)}, u32[]{:S(2)}, u32[]{:S(2)}) collective-permute-start(f32[2,2,16,32,128]{4,3,2,1,0:T(8,128)S(1)} %bitcast.249), channel_id=1, source_target_pairs={{0,4},{1,5},{2,6},{3,7},{4,0},{5,1},{6,2},{7,3},{8,12},{9,13},{10,... | collective-permute-start | bytes 3145736 | tf_op jit(solution)/shard_map/ppermute | solution.py:107
  469.3 158.9 %collective-permute-start.7 = (f32[2,2,16,32,128]{4,3,2,1,0:T(8,128)S(1)}, f32[2,2,16,32,128]{4,3,2,1,0:T(8,128)S(1)}, u32[]{:S(2)}, u32[]{:S(2)}) collective-permute-start(f32[2,2,16,32,128]{4,3,2,1,0:T(8,128)S(1)} %bitcast.248), channel_id=1, source_target_pairs={{0,6},{1,7},{2,0},{3,1},{4,2},{5,3},{6,4},{7,5},{8,14},{9,15},{10,... | collective-permute-start | bytes 3145736 | tf_op jit(solution)/shard_map/ppermute | solution.py:107
  471.6 157.6 %collective-permute-start.8 = (f32[2,2,16,32,128]{4,3,2,1,0:T(8,128)S(1)}, f32[2,2,16,32,128]{4,3,2,1,0:T(8,128)S(1)}, u32[]{:S(2)}, u32[]{:S(2)}) collective-permute-start(f32[2,2,16,32,128]{4,3,2,1,0:T(8,128)S(1)} %bitcast.247), channel_id=1, source_target_pairs={{0,7},{1,0},{2,1},{3,2},{4,3},{5,4},{6,5},{7,6},{8,15},{9,8},{10,9... | collective-permute-start | bytes 3145736 | tf_op jit(solution)/shard_map/ppermute | solution.py:107
  649.5 4.5 copy-start.2
  649.5 4.5 copy-start.15
  654.0 3.6 copy-start.14
  657.6 3.4 copy-start.13
  666.0 4.9 copy-start.12
  670.9 5.4 copy-start.3
  670.9 5.4 copy-start.11
  676.3 3.4 copy-start.10
  689.8 4.9 copy-start.5
  712.7 68.0 %collective-permute-start.9 = (f32[2,2,16,23,1024]{4,2,3,1,0:T(8,128)S(1)}, f32[2,2,16,23,1024]{4,2,3,1,0:T(8,128)S(1)}, u32[]{:S(2)}, u32[]{:S(2)}) collective-permute-start(f32[2,2,16,23,1024]{4,2,3,1,0:T(8,128)S(1)} %copy.122), channel_id=1, source_target_pairs={{0,8},{8,16},{16,24},{1,9},{9,17},{17,25},{2,10},{10,18},{18,26},{... | collective-permute-start | bytes 18087944 | tf_op jit(solution)/shard_map/ppermute | solution.py:31
  719.1 69.5 %collective-permute-start.10 = (f32[2,2,16,23,1024]{4,2,3,1,0:T(8,128)S(1)}, f32[2,2,16,23,1024]{4,2,3,1,0:T(8,128)S(1)}, u32[]{:S(2)}, u32[]{:S(2)}) collective-permute-start(f32[2,2,16,23,1024]{4,2,3,1,0:T(8,128)S(1)} %copy.123), channel_id=1, source_target_pairs={{8,0},{16,8},{24,16},{9,1},{17,9},{25,17},{10,2},{18,10},{26,18},{... | collective-permute-start | bytes 18087944 | tf_op jit(solution)/shard_map/ppermute | solution.py:32
  794.8 8.4 %copy-start.17 = (f32[32,78]{1,0:T(8,128)S(1)}, f32[32,78]{1,0:T(8,128)}, u32[]{:S(2)}) copy-start(f32[32,78]{1,0:T(8,128)} %get-tuple-element.15) | copy-start | bytes 29956
  803.3 12.3 %copy-start.1 = (f32[2,16,32,1024]{3,2,1,0:T(8,128)S(1)}, f32[2,16,32,1024]{3,2,1,0:T(8,128)}, u32[]{:S(2)}) copy-start(f32[2,16,32,1024]{3,2,1,0:T(8,128)} %param.5) | copy-start | bytes 12582916
  803.3 12.3 %copy-start.16 = (f32[32,78]{1,0:T(8,128)S(1)}, f32[32,78]{1,0:T(8,128)}, u32[]{:S(2)}) copy-start(f32[32,78]{1,0:T(8,128)} %get-tuple-element.70) | copy-start | bytes 29956
